TPU v7x, 256 devices: a whole 4x4x8 slice. The times are simulated.
256 devices in a mesh: wall: 16 (over y, x_lo, core), span: 16 (over x_hi, z).
Axes of the slice: x: 4 (x_hi: 2, x_lo: 2; x = x_hi * 2 + x_lo), y: 4, z: 8, core: 2. Of those that a mesh axis runs over, the one named last changes fastest.
Arguments:
- field: float32 [4, 3, 2, 512, 6144], P(None, None, None, 'wall', 'span'), may hold values from -6 to 6
- mean_flow: float32 [2, 512], P(None, 'wall'), may hold values from 0.2 to 1.5
- d2_coef: float32 [15, 512], P(None, 'wall'), may hold values from -2 to 2
- wall_coef: float32 [2, 8], replicated, may hold values from -0.4375 to 0.4375
- kx_index: int32 [4], replicated, may hold values from 1 to 7
- patch_of: int32 [6144], P('span'), may hold values from 0 to 63
Outputs:
- new_field: float32 [4, 3, 2, 512, 6144], P(None, None, None, 'wall', 'span')
- wall_grad: float32 [2, 4, 2, 64], replicated
All inputs are finite; a program needn't handle non-finite values.
Results may differ from a plain program's by a relative error of at most 0.000073.
Values sent between devices are 32-bit elements; how exact they have to be, the bound alone decides.
A program may use at most 128 MiB of HBM per device.

v0:
```python
import math
import jax
import jax.numpy as jnp
from jax import lax
from jax.sharding import PartitionSpec as P

HALO = 7
STEN = 15
PATCH = 64
TAU = 0.25
VIS = 0.5


def with_halo(block, sides, width):
    for axis, dim in sides:
        count = lax.axis_size(axis)
        forward = [(i, i + 1) for i in range(count - 1)]
        backward = [(target, source) for source, target in forward]
        low = lax.ppermute(
            lax.slice_in_dim(block, block.shape[dim] - width, None, axis=dim), axis, forward
        )
        high = lax.ppermute(lax.slice_in_dim(block, 0, width, axis=dim), axis, backward)
        block = jnp.concatenate([low, block, high], axis=dim)
    return block


def spanwise_operator(line_data):
    item_count, part_count, row_count, length = line_data.shape
    inner_size = 128
    outer_size = length // inner_size
    highest = lax.Precision.HIGHEST
    real_part = line_data[:, 0].reshape(item_count, row_count, outer_size, inner_size)
    imag_part = line_data[:, 1].reshape(item_count, row_count, outer_size, inner_size)
    outer = jnp.arange(outer_size, dtype=jnp.int32)
    inner = jnp.arange(inner_size, dtype=jnp.int32)
    angle_one = (
        -2.0
        * math.pi
        / outer_size
        * (outer[:, None] * outer[None, :] % outer_size).astype(jnp.float32)
    )
    angle_two = (
        -2.0
        * math.pi
        / inner_size
        * (inner[:, None] * inner[None, :] % inner_size).astype(jnp.float32)
    )
    angle_twist = (
        -2.0 * math.pi / length * (outer[:, None] * inner[None, :] % length).astype(jnp.float32)
    )
    cos_one, sin_one = (jnp.cos(angle_one), jnp.sin(angle_one))
    cos_two, sin_two = (jnp.cos(angle_two), jnp.sin(angle_two))
    cos_twist, sin_twist = (jnp.cos(angle_twist), jnp.sin(angle_twist))

    def first_section(table, values):
        return jnp.einsum("kn,irnm->irkm", table, values, precision=highest)

    def second_section(values, table):
        return jnp.einsum("irkn,nm->irkm", values, table, precision=highest)

    def second_back(values, table):
        return jnp.einsum("irkm,nm->irkn", values, table, precision=highest)

    def first_back(table, values):
        return jnp.einsum("kn,irkm->irnm", table, values, precision=highest)

    section_real = first_section(cos_one, real_part) - first_section(sin_one, imag_part)
    section_imag = first_section(cos_one, imag_part) + first_section(sin_one, real_part)
    twist_real = section_real * cos_twist - section_imag * sin_twist
    twist_imag = section_real * sin_twist + section_imag * cos_twist
    modes_real = second_section(twist_real, cos_two) - second_section(twist_imag, sin_two)
    modes_imag = second_section(twist_real, sin_two) + second_section(twist_imag, cos_two)
    wave_index = outer[:, None] + outer_size * inner[None, :]
    signed = jnp.where(wave_index > length // 2, wave_index - length, wave_index)
    cutoff = length // 3
    wave_ratio = signed.astype(jnp.float32) / cutoff
    multiplier = jnp.where(
        jnp.abs(signed) < cutoff, -VIS * wave_ratio * wave_ratio, 0.0 * wave_ratio
    )
    modes_real = modes_real * multiplier
    modes_imag = modes_imag * multiplier
    back_real = second_back(modes_real, cos_two) + second_back(modes_imag, sin_two)
    back_imag = second_back(modes_imag, cos_two) - second_back(modes_real, sin_two)
    untwist_real = back_real * cos_twist + back_imag * sin_twist
    untwist_imag = back_imag * cos_twist - back_real * sin_twist
    result_real = (first_back(cos_one, untwist_real) + first_back(sin_one, untwist_imag)) / length
    result_imag = (first_back(cos_one, untwist_imag) - first_back(sin_one, untwist_real)) / length
    result_real = result_real.reshape(item_count, row_count, length)
    result_imag = result_imag.reshape(item_count, row_count, length)
    return jnp.stack([result_real, result_imag], axis=1)


def on_device(field, mean_flow, d2_coef, wall_coef, kx_index, patch_of):
    mode_count, comp_count, part_count, row_count, col_count = field.shape
    padded = with_halo(field, (("wall", 3),), HALO)
    diffusion = jnp.zeros_like(field)
    for offset in range(STEN):
        diffusion = (
            diffusion + d2_coef[offset][:, None] * padded[:, :, :, offset : offset + row_count, :]
        )
    flattened = field.reshape(mode_count * comp_count, part_count, row_count, col_count)
    spectral_lines = spanwise_operator(
        lax.all_to_all(flattened, "span", split_axis=2, concat_axis=3, tiled=True)
    )
    spanwise = lax.all_to_all(spectral_lines, "span", split_axis=3, concat_axis=2, tiled=True)
    spanwise = spanwise.reshape(field.shape)
    wave_number = kx_index.astype(jnp.float32) * 0.25
    velocity = mean_flow[0]
    shear_rate = mean_flow[1]
    advect_rate = wave_number[:, None, None, None] * velocity[None, None, :, None]
    advect_real = -advect_rate * field[:, :, 1]
    advect_imag = advect_rate * field[:, :, 0]
    advection = jnp.stack([advect_real, advect_imag], axis=2)
    coupling = shear_rate[None, None, :, None] * field[:, 0]
    advection = advection.at[:, 1].add(-coupling)
    new_field = field + TAU * advection + diffusion + spanwise
    lower_wall = jnp.zeros_like(new_field[:, 0, :, 0, :])
    upper_wall = jnp.zeros_like(new_field[:, 0, :, 0, :])
    for offset in range(HALO + 1):
        lower_wall = lower_wall + wall_coef[0, offset] * new_field[:, 0, :, offset, :]
        upper_wall = (
            upper_wall + wall_coef[1, offset] * new_field[:, 0, :, row_count - 1 - offset, :]
        )
    wall_index = lax.axis_index("wall")
    wall_count = lax.axis_size("wall")
    lower_wall = jnp.where(wall_index == 0, lower_wall, 0.0 * lower_wall)
    upper_wall = jnp.where(wall_index == wall_count - 1, upper_wall, 0.0 * upper_wall)
    shear_rows = jnp.stack([lower_wall, upper_wall])
    onehot = (patch_of[:, None] == jnp.arange(PATCH, dtype=jnp.int32)[None, :]).astype(jnp.float32)
    partial_grad = jnp.einsum("wmcz,zp->wmcp", shear_rows, onehot, precision=lax.Precision.HIGHEST)
    wall_grad = lax.psum(partial_grad, ("wall", "span"))
    return (new_field, wall_grad)


def solution(mesh):
    return jax.shard_map(
        on_device,
        mesh=mesh,
        in_specs=(
            P(None, None, None, "wall", "span"),
            P(None, "wall"),
            P(None, "wall"),
            P(),
            P(),
            P("span"),
        ),
        out_specs=(P(None, None, None, "wall", "span"), P()),
        check_vma=False,
    )
```

profile of v0, /device:TPU:1, one launch (start us, length us, event | category | flops | bytes accessed | tf_op | source)
XLA Modules:
  0.0 284.4 jit_solution(1954556570748203936)
XLA Ops:
  0.6 3.2 %copy.115 = f32[4,3,2,32,384]{4,2,1,0,3:T(2,128)} copy(f32[4,3,2,32,384]{4,3,2,1,0:T(8,128)} %param.8) | data formatting | bytes 2359296 | tf_op args[0]
  3.8 11.7 %all-to-all-start = ((f32[12,2,32,384]{3,1,0,2:T(2,128)}), f32[12,2,32,384]{3,1,0,2:T(2,128)S(1)}, u32[]{:S(2)}, u32[]{:S(2)}) async-start(f32[12,2,32,384]{3,1,0,2:T(2,128)} %bitcast.18), calls=%async_computation | async-start | bytes 2359296 | tf_op jit(solution)/shard_map/all_to_all | solution.py:103
  15.6 0.8 copy.109
  16.3 0.9 fusion.198
  17.2 3.0 %collective-permute-start = (f32[4,3,2,7,384]{4,0,2,3,1:T(4,128)}, f32[4,3,2,7,384]{4,0,2,3,1:T(4,128)}, u32[]{:S(2)}, u32[]{:S(2)}) collective-permute-start(f32[4,3,2,7,384]{4,0,2,3,1:T(4,128)} %get-tuple-element.32), channel_id=1, source_target_pairs={{0,16},{16,32},{32,48},{48,64},{64,80},{80,96},{96,112},{112,128},... | collective-permute-start | bytes 774152 | tf_op jit(solution)/shard_map/ppermute | solution.py:19
  20.3 2.0 collective-permute-start.1
  22.3 0.7 fusion.83
  23.0 0.6 multiply_select_fusion
  23.6 21.4 %all-to-all-done = f32[12,2,32,384]{3,1,0,2:T(2,128)S(1)} async-done(((f32[12,2,32,384]{3,1,0,2:T(2,128)}), f32[12,2,32,384]{3,1,0,2:T(2,128)S(1)}, u32[]{:S(2)}, u32[]{:S(2)}) %all-to-all-start) | async-done | bytes 1179680 | tf_op jit(solution)/shard_map/all_to_all | solution.py:103
  45.0 1.4 copy.116
  46.4 2.1 all_to_all.27
  49.1 0.8 fusion.77
  50.4 0.8 fusion.79
  51.1 0.8 convolution_add_fusion.3
  51.9 0.8 convolution_subtract_fusion.3
  52.7 0.9 fusion.24
  53.6 0.9 fusion.26
  54.5 0.9 fusion.4
  55.4 0.9 fusion.40
  56.3 0.9 fusion.5
  57.2 0.9 fusion.43
  58.0 0.9 convolution_subtract_fusion.1
  58.9 0.9 convolution_add_fusion.1
  59.8 0.8 fusion.32
  60.6 1.0 fusion.33
  61.7 0.8 fusion.3
  62.5 4.5 %copy.141 = f32[12,2,48,128]{0,1,3,2:T(2,128)} copy(f32[12,2,48,128]{3,2,1,0:T(8,128)S(1)} %fusion.3) | data formatting | bytes 1179648 | tf_op jit(solution)/shard_map/stack;reshape | solution.py:90
  67.0 1.6 fusion.1
  68.6 4.6 %copy.142 = f32[12,2,48,128]{0,1,3,2:T(2,128)} copy(f32[12,2,48,128]{3,2,1,0:T(8,128)S(1)} %fusion.1) | data formatting | bytes 1179648 | tf_op jit(solution)/shard_map/stack;reshape | solution.py:90
  73.2 11.8 %fusion.200 = f32[6144,2,2,12]{3,2,1,0:T(2,128)} fusion(f32[12,1,2,6144]{0,2,1,3:T(2,128)} %bitcast.155, f32[12,1,2,6144]{0,2,1,3:T(2,128)} %bitcast.154), kind=kLoop, calls=%fused_computation.261 | loop fusion | flops 294912 | bytes 2359296
  85.0 22.7 %reshape.465 = f32[16,1,18432]{2,1,0:T(1,128)} reshape(f32[6144,2,2,12]{3,2,1,0:T(2,128)} %fusion.200) | data formatting | bytes 2359296
  107.7 6.6 %all-to-all-start.1 = ((f32[16,1,18432]{2,1,0:T(1,128)}), f32[16,1,18432]{2,1,0:T(1,128)}, u32[]{:S(2)}, u32[]{:S(2)}) async-start(f32[16,1,18432]{2,1,0:T(1,128)} %reshape.465), calls=%async_computation.1 | async-start | bytes 2359296 | tf_op jit(solution)/shard_map/all_to_all | solution.py:105
  116.5 0.7 fusion.199
  117.3 1.0 fusion.30
  118.3 1.0 copy-done.3
  119.3 1.0 constant_dynamic-update-slice_fusion.1
  120.2 1.0 constant_dynamic-update-slice_fusion
  121.3 1.0 constant_dynamic-update-slice_fusion.2
  122.3 21.7 %all-to-all-done.1 = f32[16,1,18432]{2,1,0:T(1,128)} async-done(((f32[16,1,18432]{2,1,0:T(1,128)}), f32[16,1,18432]{2,1,0:T(1,128)}, u32[]{:S(2)}, u32[]{:S(2)}) %all-to-all-start.1) | async-done | bytes 1179680 | tf_op jit(solution)/shard_map/all_to_all | solution.py:105
  144.5 5.7 %reduce.2 = f32[16,18432]{1,0:T(8,128)} reduce(f32[16,1,18432]{2,1,0:T(1,128)} %all-to-all-done.1, f32[]{:T(128)} %broadcast.394), dimensions={1}, to_apply=%all_to_all.28.reduce_sub_computation | reduce | bytes 2359300 | tf_op jit(solution)/shard_map/all_to_all | solution.py:105
  150.2 27.5 %reshape.466 = f32[6144,2,2,12]{3,2,1,0:T(2,128)} reshape(f32[16,18432]{1,0:T(8,128)} %reduce.2) | data formatting | bytes 2359296
  177.7 11.2 %copy.143 = f32[12,2,2,16,384]{4,3,2,1,0:T(8,128)} copy(f32[12,2,2,16,384]{0,2,1,4,3:T(2,128)} %bitcast.153) | data formatting | bytes 2359296 | tf_op jit(solution)/shard_map/all_to_all | solution.py:105
  188.9 2.3 copy.124
  191.4 4.5 %fusion.8 = f32[4,3,2,32,384]{4,0,2,3,1:T(4,128)S(1)} fusion(f32[4,3,2,39,384]{4,0,2,3,1:T(4,128)S(1)} %constant_dynamic-update-slice_fusion.2, f32[4,3,2,39,384]{4,0,2,3,1:T(4,128)S(1)} %get-tuple-element.30, f32[4,3,2,32,384]{4,2,3,1,0:T(2,128)S(1)} %bitcast.156, f32[4,3,2,32,384]{4,0,2,3,1:T(4,128)S(1)} %copy-done.4, f32[32]{0:T(128)S(1)} %copy-done.19, ...), kind=kLoop, calls=%fused_computation.21 | loop fusion | flops 9732096 | bytes 21235584 | tf_op jit(solution)/shard_map/add | solution.py:116
  195.9 1.2 copy.126
  197.1 5.2 %multiply_select_fusion.1 = f32[1,4,2,384]{3,1,2,0:T(4,128)S(1)} fusion(f32[4,3,2,32,384]{4,0,2,3,1:T(4,128)S(1)} %fusion.8, f32[]{:T(128)} %bitcast.61, f32[]{:T(128)} %bitcast.60, f32[]{:T(128)} %bitcast.59, f32[]{:T(128)} %bitcast.58, f32[]{:T(128)} %bitcast.57, f32[]{:T(128)} %bitcast.56, f32[]{:T(128)} %bitcast.55, f32[]{:T(128)} %bitcast.54, pred[]{:T(512)S(6)} %eq.26), kind=kLoop, calls=%fused_computation.126 | loop fusion | flops 52224 | bytes 110625 | tf_op jit(solution)/shard_map/jit(_where)/select_n | solution.py:127
  202.4 5.1 %multiply_select_fusion.2 = f32[1,4,2,384]{3,1,2,0:T(4,128)S(1)} fusion(f32[4,3,2,32,384]{4,0,2,3,1:T(4,128)S(1)} %fusion.8, f32[]{:T(128)} %bitcast.52, f32[]{:T(128)} %bitcast.51, f32[]{:T(128)} %bitcast.50, f32[]{:T(128)} %bitcast.49, f32[]{:T(128)} %bitcast.48, f32[]{:T(128)} %bitcast.47, f32[]{:T(128)} %bitcast.46, f32[]{:T(128)} %bitcast.45, pred[]{:T(512)S(6)} %eq.25), kind=kLoop, calls=%fused_computation.127 | loop fusion | flops 52224 | bytes 110625 | tf_op jit(solution)/shard_map/jit(_where)/select_n | solution.py:126
  207.7 76.1 %psum.7 = f32[2,4,2,64]{3,1,2,0:T(4,128)S(1)} all-reduce(f32[2,4,2,64]{3,1,2,0:T(4,128)S(1)} %fusion.35), channel_id=1, replica_groups=mesh['wall'=16,'span'=16] {'wall','span'}, use_global_device_ids=true, to_apply=%region_0.1 | all-reduce | flops 1024 | bytes 8192 | tf_op jit(solution)/shard_map/psum | solution.py:131
  (62 shorter events, 4.6 us)
Async XLA Ops:
  3.8 11.7 %copy-start = (f32[4,3,2,32,384]{4,3,2,1,0:T(8,128)S(1)}, f32[4,3,2,32,384]{4,3,2,1,0:T(8,128)}, u32[]{:S(2)}) copy-start(f32[4,3,2,32,384]{4,3,2,1,0:T(8,128)} %param.8) | copy-start | bytes 3538948
  3.8 41.2 %all-to-all-start = ((f32[12,2,32,384]{3,1,0,2:T(2,128)}), f32[12,2,32,384]{3,1,0,2:T(2,128)S(1)}, u32[]{:S(2)}, u32[]{:S(2)}) async-start(f32[12,2,32,384]{3,1,0,2:T(2,128)} %bitcast.18), calls=%async_computation | async-start | bytes 2359296 | tf_op jit(solution)/shard_map/all_to_all | solution.py:103
  17.2 101.0 %collective-permute-start = (f32[4,3,2,7,384]{4,0,2,3,1:T(4,128)}, f32[4,3,2,7,384]{4,0,2,3,1:T(4,128)}, u32[]{:S(2)}, u32[]{:S(2)}) collective-permute-start(f32[4,3,2,7,384]{4,0,2,3,1:T(4,128)} %get-tuple-element.32), channel_id=1, source_target_pairs={{0,16},{16,32},{32,48},{48,64},{64,80},{80,96},{96,112},{112,128},... | collective-permute-start | bytes 774152 | tf_op jit(solution)/shard_map/ppermute | solution.py:19
  20.3 101.0 %collective-permute-start.1 = (f32[4,3,2,7,384]{4,0,2,3,1:T(4,128)}, f32[4,3,2,7,384]{4,0,2,3,1:T(4,128)}, u32[]{:S(2)}, u32[]{:S(2)}) collective-permute-start(f32[4,3,2,7,384]{4,0,2,3,1:T(4,128)} %get-tuple-element.33), channel_id=1, source_target_pairs={{16,0},{32,16},{48,32},{64,48},{80,64},{96,80},{112,96},{128,112},... | collective-permute-start | bytes 774152 | tf_op jit(solution)/shard_map/ppermute | solution.py:22
  51.9 0.8 copy-start.5
  51.9 0.8 copy-start.6
  53.6 0.9 copy-start.7
  107.7 6.7 %copy-start.23 = (s32[4]{0:T(128)S(1)}, s32[4]{0:T(128)}, u32[]{:S(2)}) copy-start(s32[4]{0:T(128)} %param.12) | copy-start | bytes 52
  107.7 6.7 %copy-start.21 = (f32[2,32]{1,0:T(2,128)S(1)}, f32[2,32]{1,0:T(2,128)}, u32[]{:S(2)}) copy-start(f32[2,32]{1,0:T(2,128)} %param.9) | copy-start | bytes 772
  107.7 36.3 %all-to-all-start.1 = ((f32[16,1,18432]{2,1,0:T(1,128)}), f32[16,1,18432]{2,1,0:T(1,128)}, u32[]{:S(2)}, u32[]{:S(2)}) async-start(f32[16,1,18432]{2,1,0:T(1,128)} %reshape.465), calls=%async_computation.1 | async-start | bytes 2359296 | tf_op jit(solution)/shard_map/all_to_all | solution.py:105
  115.2 0.7 copy-start.9
  115.2 1.3 copy-start.8
  117.3 3.0 %copy-start.1 = (f32[4,3,2,32,384]{4,3,2,1,0:T(8,128)S(1)}, f32[4,3,2,32,384]{4,3,2,1,0:T(8,128)}, u32[]{:S(2)}) copy-start(f32[4,3,2,32,384]{4,3,2,1,0:T(8,128)} %param.8) | copy-start | bytes 3538948
  118.2 1.0 copy-start.3
  188.8 2.4 copy-start.2
  188.8 2.4 copy-start.4
  188.8 2.5 copy-start.10
  188.8 2.5 copy-start.11
  188.9 2.5 copy-start.12
  188.9 2.5 copy-start.13
  188.9 2.5 copy-start.14
  188.9 2.5 copy-start.15
  188.9 2.5 copy-start.16
  188.9 2.5 copy-start.17
  188.9 2.5 copy-start.18
  188.9 2.5 copy-start.19
  188.9 2.5 copy-start.20
  195.9 11.6 %copy-start.22 = (s32[384]{0:T(512)S(1)}, s32[384]{0:T(512)}, u32[]{:S(2)}) copy-start(s32[384]{0:T(512)} %param.13) | copy-start | bytes 4612
where the time goes:
time: 286 us; the launch traced here: 284 us
  local copies, waits for them, and re-layouts  90.8 us (32%)
  blocking collectives  76.1 us (27%)
  waiting for transfers between devices  43.1 us (15%)
  other arithmetic  35.3 us (12%)
  starting transfers between devices  23.4 us (8%)
  matrix products  14.5 us (5%)
    psum x1, blocking collectives, on_device(): wall_grad = lax.psum(partial_grad, ('wall', 'span'))  76.1 us
    unnamed x55, local copies, waits for them, and re-layouts  58.4 us
    all_to_all x1, waiting for transfers between devices, on_device(): lax.all_to_all(spectral_lines, 'span', split_axis=3, concat_axis=2, tiled...  21.7 us
    all_to_all x1, waiting for transfers between devices, on_device(): lax.all_to_all(flattened, 'span', split_axis=2, concat_axis=3, tiled=True)  21.4 us
    all_to_all x3, local copies, waits for them, and re-layouts, on_device(): lax.all_to_all(spectral_lines, 'span', split_axis=3, concat_axis=2, tiled...  14 us
    unnamed x1, other arithmetic  11.8 us
    all_to_all x1, starting transfers between devices, on_device(): lax.all_to_all(flattened, 'span', split_axis=2, concat_axis=3, tiled=True)  11.7 us
    another operation x2, local copies, waits for them, and re-layouts, spanwise_operator(): return jnp.stack([result_real, result_imag], axis=1)  9.1 us
  transfers between devices with their start and end apart: 4, of which 2 were waited for; matrix products, arithmetic and copies ran while one was open for 25% of the time, Pallas kernels for 0%

commit v1 on v0

--- a/solution.py
+++ b/solution.py
@@ -128,7 +128,9 @@
     shear_rows = jnp.stack([lower_wall, upper_wall])
     onehot = (patch_of[:, None] == jnp.arange(PATCH, dtype=jnp.int32)[None, :]).astype(jnp.float32)
     partial_grad = jnp.einsum("wmcz,zp->wmcp", shear_rows, onehot, precision=lax.Precision.HIGHEST)
-    wall_grad = lax.psum(partial_grad, ("wall", "span"))
+    wall_grad = partial_grad
+    for over in ("wall", "span"):
+        wall_grad = lax.psum(wall_grad, over)
     return (new_field, wall_grad)
 
 

time: 286 us -> 277 us (0.969)
  the two profiles are of different devices: /device:TPU:1 before, /device:TPU:4 now
where the time goes in v1:
time: 277 us; the launch traced here: 275 us
  local copies, waits for them, and re-layouts  90.9 us (33%)
  blocking collectives  68.4 us (25%)
  waiting for transfers between devices  42.9 us (15%)
  other arithmetic  35.2 us (13%)
  starting transfers between devices  22.3 us (8%)
  matrix products  14.5 us (5%)
    psum x2, blocking collectives, on_device(): wall_grad = lax.psum(wall_grad, over)  68.4 us
    unnamed x55, local copies, waits for them, and re-layouts  58.5 us
    all_to_all x1, waiting for transfers between devices, on_device(): lax.all_to_all(flattened, 'span', split_axis=2, concat_axis=3, tiled=True)  22.1 us
    all_to_all x1, waiting for transfers between devices, on_device(): lax.all_to_all(spectral_lines, 'span', split_axis=3, concat_axis=2, tiled...  20.8 us
    all_to_all x3, local copies, waits for them, and re-layouts, on_device(): lax.all_to_all(spectral_lines, 'span', split_axis=3, concat_axis=2, tiled...  14 us
    unnamed x1, other arithmetic  11.8 us
    all_to_all x1, starting transfers between devices, on_device(): lax.all_to_all(flattened, 'span', split_axis=2, concat_axis=3, tiled=True)  11.6 us
    another operation x2, local copies, waits for them, and re-layouts, spanwise_operator(): return jnp.stack([result_real, result_imag], axis=1)  9.11 us
  transfers between devices with their start and end apart: 4, of which 2 were waited for; matrix products, arithmetic and copies ran while one was open for 25% of the time, Pallas kernels for 0%

profile of v1, /device:TPU:4, one launch (start us, length us, event | category | flops | bytes accessed | tf_op | source)
XLA Modules:
  0.0 275.4 jit_solution(792947561176193262)
XLA Ops:
  0.6 3.2 %copy.115 = f32[4,3,2,32,384]{4,2,1,0,3:T(2,128)} copy(f32[4,3,2,32,384]{4,3,2,1,0:T(8,128)} %param.8) | data formatting | bytes 2359296 | tf_op args[0]
  3.8 11.6 %all-to-all-start = ((f32[12,2,32,384]{3,1,0,2:T(2,128)}), f32[12,2,32,384]{3,1,0,2:T(2,128)S(1)}, u32[]{:S(2)}, u32[]{:S(2)}) async-start(f32[12,2,32,384]{3,1,0,2:T(2,128)} %bitcast.18), calls=%async_computation | async-start | bytes 2359296 | tf_op jit(solution)/shard_map/all_to_all | solution.py:103
  15.4 0.8 copy.109
  16.2 0.9 fusion.198
  17.1 2.0 collective-permute-start
  19.1 1.3 collective-permute-start.1
  20.4 0.7 fusion.83
  21.8 22.1 %all-to-all-done = f32[12,2,32,384]{3,1,0,2:T(2,128)S(1)} async-done(((f32[12,2,32,384]{3,1,0,2:T(2,128)}), f32[12,2,32,384]{3,1,0,2:T(2,128)S(1)}, u32[]{:S(2)}, u32[]{:S(2)}) %all-to-all-start) | async-done | bytes 1179680 | tf_op jit(solution)/shard_map/all_to_all | solution.py:103
  43.9 1.4 copy.116
  45.3 2.1 all_to_all.27
  47.9 0.8 fusion.77
  49.2 0.8 fusion.79
  50.0 0.8 convolution_add_fusion.3
  50.8 0.8 convolution_subtract_fusion.3
  51.6 0.9 fusion.24
  52.5 0.9 fusion.26
  53.4 0.9 fusion.4
  54.2 0.9 fusion.40
  55.1 0.9 fusion.5
  56.0 0.9 fusion.43
  56.9 0.9 convolution_subtract_fusion.1
  57.8 0.9 convolution_add_fusion.1
  58.6 0.8 fusion.32
  59.5 1.0 fusion.33
  60.5 0.8 fusion.3
  61.4 4.5 %copy.141 = f32[12,2,48,128]{0,1,3,2:T(2,128)} copy(f32[12,2,48,128]{3,2,1,0:T(8,128)S(1)} %fusion.3) | data formatting | bytes 1179648 | tf_op jit(solution)/shard_map/stack;reshape | solution.py:90
  65.9 1.6 fusion.1
  67.5 4.6 %copy.142 = f32[12,2,48,128]{0,1,3,2:T(2,128)} copy(f32[12,2,48,128]{3,2,1,0:T(8,128)S(1)} %fusion.1) | data formatting | bytes 1179648 | tf_op jit(solution)/shard_map/stack;reshape | solution.py:90
  72.1 11.8 %fusion.200 = f32[6144,2,2,12]{3,2,1,0:T(2,128)} fusion(f32[12,1,2,6144]{0,2,1,3:T(2,128)} %bitcast.155, f32[12,1,2,6144]{0,2,1,3:T(2,128)} %bitcast.154), kind=kLoop, calls=%fused_computation.261 | loop fusion | flops 294912 | bytes 2359296
  83.8 22.7 %reshape.465 = f32[16,1,18432]{2,1,0:T(1,128)} reshape(f32[6144,2,2,12]{3,2,1,0:T(2,128)} %fusion.200) | data formatting | bytes 2359296
  106.5 7.4 %all-to-all-start.1 = ((f32[16,1,18432]{2,1,0:T(1,128)}), f32[16,1,18432]{2,1,0:T(1,128)}, u32[]{:S(2)}, u32[]{:S(2)}) async-start(f32[16,1,18432]{2,1,0:T(1,128)} %reshape.465), calls=%async_computation.1 | async-start | bytes 2359296 | tf_op jit(solution)/shard_map/all_to_all | solution.py:105
  116.2 0.7 fusion.199
  116.9 1.0 fusion.30
  117.9 1.0 copy-done.3
  119.0 1.0 constant_dynamic-update-slice_fusion.1
  119.9 1.0 constant_dynamic-update-slice_fusion
  121.0 1.0 constant_dynamic-update-slice_fusion.2
  122.0 20.8 %all-to-all-done.1 = f32[16,1,18432]{2,1,0:T(1,128)} async-done(((f32[16,1,18432]{2,1,0:T(1,128)}), f32[16,1,18432]{2,1,0:T(1,128)}, u32[]{:S(2)}, u32[]{:S(2)}) %all-to-all-start.1) | async-done | bytes 1179680 | tf_op jit(solution)/shard_map/all_to_all | solution.py:105
  143.3 5.7 %reduce.2 = f32[16,18432]{1,0:T(8,128)} reduce(f32[16,1,18432]{2,1,0:T(1,128)} %all-to-all-done.1, f32[]{:T(128)} %broadcast.394), dimensions={1}, to_apply=%all_to_all.28.reduce_sub_computation | reduce | bytes 2359300 | tf_op jit(solution)/shard_map/all_to_all | solution.py:105
  149.0 27.5 %reshape.466 = f32[6144,2,2,12]{3,2,1,0:T(2,128)} reshape(f32[16,18432]{1,0:T(8,128)} %reduce.2) | data formatting | bytes 2359296
  176.5 11.2 %copy.143 = f32[12,2,2,16,384]{4,3,2,1,0:T(8,128)} copy(f32[12,2,2,16,384]{0,2,1,4,3:T(2,128)} %bitcast.153) | data formatting | bytes 2359296 | tf_op jit(solution)/shard_map/all_to_all | solution.py:105
  187.7 2.3 copy.124
  190.2 4.5 %fusion.8 = f32[4,3,2,32,384]{4,0,2,3,1:T(4,128)S(1)} fusion(f32[4,3,2,39,384]{4,0,2,3,1:T(4,128)S(1)} %constant_dynamic-update-slice_fusion.2, f32[4,3,2,39,384]{4,0,2,3,1:T(4,128)S(1)} %get-tuple-element.30, f32[4,3,2,32,384]{4,2,3,1,0:T(2,128)S(1)} %bitcast.156, f32[4,3,2,32,384]{4,0,2,3,1:T(4,128)S(1)} %copy-done.4, f32[32]{0:T(128)S(1)} %copy-done.19, ...), kind=kLoop, calls=%fused_computation.21 | loop fusion | flops 9732096 | bytes 21235584 | tf_op jit(solution)/shard_map/add | solution.py:116
  194.7 1.2 copy.126
  195.9 5.2 %multiply_select_fusion.1 = f32[1,4,2,384]{3,1,2,0:T(4,128)S(1)} fusion(f32[4,3,2,32,384]{4,0,2,3,1:T(4,128)S(1)} %fusion.8, f32[]{:T(128)} %bitcast.61, f32[]{:T(128)} %bitcast.60, f32[]{:T(128)} %bitcast.59, f32[]{:T(128)} %bitcast.58, f32[]{:T(128)} %bitcast.57, f32[]{:T(128)} %bitcast.56, f32[]{:T(128)} %bitcast.55, f32[]{:T(128)} %bitcast.54, pred[]{:T(512)S(6)} %eq.26), kind=kLoop, calls=%fused_computation.126 | loop fusion | flops 52224 | bytes 110625 | tf_op jit(solution)/shard_map/jit(_where)/select_n | solution.py:127
  201.1 5.0 %multiply_select_fusion.2 = f32[1,4,2,384]{3,1,2,0:T(4,128)S(1)} fusion(f32[4,3,2,32,384]{4,0,2,3,1:T(4,128)S(1)} %fusion.8, f32[]{:T(128)} %bitcast.52, f32[]{:T(128)} %bitcast.51, f32[]{:T(128)} %bitcast.50, f32[]{:T(128)} %bitcast.49, f32[]{:T(128)} %bitcast.48, f32[]{:T(128)} %bitcast.47, f32[]{:T(128)} %bitcast.46, f32[]{:T(128)} %bitcast.45, pred[]{:T(512)S(6)} %eq.25), kind=kLoop, calls=%fused_computation.127 | loop fusion | flops 52224 | bytes 110625 | tf_op jit(solution)/shard_map/jit(_where)/select_n | solution.py:126
  206.4 28.1 %psum.14 = f32[2,4,2,64]{3,1,2,0:T(4,128)S(1)} all-reduce(f32[2,4,2,64]{3,1,2,0:T(4,128)S(1)} %fusion.35), channel_id=1, replica_groups=mesh['wall'=16,'span'=16] {'wall'}, use_global_device_ids=true, to_apply=%region_0.1 | all-reduce | flops 1024 | bytes 8192 | tf_op jit(solution)/shard_map/psum | solution.py:133
  234.5 40.3 %psum.15 = f32[2,4,2,64]{3,1,2,0:T(4,128)S(1)} all-reduce(f32[2,4,2,64]{3,1,2,0:T(4,128)S(1)} %psum.14), channel_id=1, replica_groups=mesh['wall'=16,'span'=16] {'span'}, use_global_device_ids=true, to_apply=%region_1.2 | all-reduce | flops 1024 | bytes 8192 | tf_op jit(solution)/shard_map/psum | solution.py:133
  (63 shorter events, 5.2 us)
Async XLA Ops:
  3.8 11.6 %copy-start = (f32[4,3,2,32,384]{4,3,2,1,0:T(8,128)S(1)}, f32[4,3,2,32,384]{4,3,2,1,0:T(8,128)}, u32[]{:S(2)}) copy-start(f32[4,3,2,32,384]{4,3,2,1,0:T(8,128)} %param.8) | copy-start | bytes 3538948
  3.8 40.1 %all-to-all-start = ((f32[12,2,32,384]{3,1,0,2:T(2,128)}), f32[12,2,32,384]{3,1,0,2:T(2,128)S(1)}, u32[]{:S(2)}, u32[]{:S(2)}) async-start(f32[12,2,32,384]{3,1,0,2:T(2,128)} %bitcast.18), calls=%async_computation | async-start | bytes 2359296 | tf_op jit(solution)/shard_map/all_to_all | solution.py:103
  17.1 100.8 %collective-permute-start = (f32[4,3,2,7,384]{4,0,2,3,1:T(4,128)}, f32[4,3,2,7,384]{4,0,2,3,1:T(4,128)}, u32[]{:S(2)}, u32[]{:S(2)}) collective-permute-start(f32[4,3,2,7,384]{4,0,2,3,1:T(4,128)} %get-tuple-element.32), channel_id=1, source_target_pairs={{0,16},{16,32},{32,48},{48,64},{64,80},{80,96},{96,112},{112,128},... | collective-permute-start | bytes 774152 | tf_op jit(solution)/shard_map/ppermute | solution.py:19
  19.1 101.9 %collective-permute-start.1 = (f32[4,3,2,7,384]{4,0,2,3,1:T(4,128)}, f32[4,3,2,7,384]{4,0,2,3,1:T(4,128)}, u32[]{:S(2)}, u32[]{:S(2)}) collective-permute-start(f32[4,3,2,7,384]{4,0,2,3,1:T(4,128)} %get-tuple-element.33), channel_id=1, source_target_pairs={{16,0},{32,16},{48,32},{64,48},{80,64},{96,80},{112,96},{128,112},... | collective-permute-start | bytes 774152 | tf_op jit(solution)/shard_map/ppermute | solution.py:22
  50.8 0.8 copy-start.5
  50.8 0.8 copy-start.6
  52.5 0.9 copy-start.7
  106.5 7.5 %copy-start.23 = (s32[4]{0:T(128)S(1)}, s32[4]{0:T(128)}, u32[]{:S(2)}) copy-start(s32[4]{0:T(128)} %param.12) | copy-start | bytes 52
  106.5 7.5 %copy-start.21 = (f32[2,32]{1,0:T(2,128)S(1)}, f32[2,32]{1,0:T(2,128)}, u32[]{:S(2)}) copy-start(f32[2,32]{1,0:T(2,128)} %param.9) | copy-start | bytes 772
  106.5 36.2 %all-to-all-start.1 = ((f32[16,1,18432]{2,1,0:T(1,128)}), f32[16,1,18432]{2,1,0:T(1,128)}, u32[]{:S(2)}, u32[]{:S(2)}) async-start(f32[16,1,18432]{2,1,0:T(1,128)} %reshape.465), calls=%async_computation.1 | async-start | bytes 2359296 | tf_op jit(solution)/shard_map/all_to_all | solution.py:105
  114.9 0.7 copy-start.9
  114.9 1.3 copy-start.8
  116.9 3.0 %copy-start.1 = (f32[4,3,2,32,384]{4,3,2,1,0:T(8,128)S(1)}, f32[4,3,2,32,384]{4,3,2,1,0:T(8,128)}, u32[]{:S(2)}) copy-start(f32[4,3,2,32,384]{4,3,2,1,0:T(8,128)} %param.8) | copy-start | bytes 3538948
  117.9 1.0 copy-start.3
  187.6 2.4 copy-start.2
  187.6 2.4 copy-start.4
  187.6 2.5 copy-start.10
  187.6 2.5 copy-start.11
  187.6 2.5 copy-start.12
  187.6 2.5 copy-start.13
  187.7 2.5 copy-start.14
  187.7 2.5 copy-start.15
  187.7 2.5 copy-start.16
  187.7 2.5 copy-start.17
  187.7 2.5 copy-start.18
  187.7 2.5 copy-start.19
  187.7 2.5 copy-start.20
  194.7 11.5 %copy-start.22 = (s32[384]{0:T(512)S(1)}, s32[384]{0:T(512)}, u32[]{:S(2)}) copy-start(s32[384]{0:T(512)} %param.13) | copy-start | bytes 4612
